TPU v7x, 256 devices: a whole 4x4x8 slice. The times are simulated.
256 devices in a mesh: row: 32 (over x, y, core), col: 8 (over z).
Axes of the slice: x: 4, y: 4, z: 8, core: 2. Of those that a mesh axis runs over, the one named last changes fastest.
Arguments:
- test_kernel: float32 [65536, 4096], P('row', 'col'), may hold values from -6 to 6
- first_panel: float32 [65536, 512], P('row', 'col'), may hold values from -0.25 to 0.25
- second_panel: float32 [65536, 512], P('row', 'col'), may hold values from -0.25 to 0.25
- first_inverse: float32 [512, 512], replicated, may hold values from -0.15 to 1.5, as said below
- second_inverse: float32 [512, 512], replicated, may hold values from -0.15 to 1.5, as said below
Outputs:
- solution: float32 [65536, 4096], P('row', 'col')
Inputs may be any that keep to these rules, and one draw needn't show every extreme that they name: `first_inverse`: lower triangular: zeros above the diagonal, diagonal entries positive. `second_inverse`: lower triangular: zeros above the diagonal, diagonal entries positive.
All inputs are finite; a program needn't handle non-finite values.
Results may differ from a plain program's by a relative error of at most 0.000075.
Values sent between devices are 32-bit elements; how exact they have to be, the bound alone decides.
A program may use at most 64 MiB of HBM per device.

v0:
```python
import jax
import jax.numpy as jnp
from jax import lax
from jax.sharding import PartitionSpec as P


def broadcast(value, axis, source):
    kept = jnp.where(lax.axis_index(axis) == source, value, 0).astype(value.dtype)
    return lax.psum(kept, axis)


def product(left, right):
    return jnp.dot(left, right, precision=lax.Precision.HIGHEST, preferred_element_type=jnp.float32)


def folding(solved, piece):
    return product(piece, solved)


def per_device(test_kernel, first_panel, second_panel, first_inverse, second_inverse):
    block = first_inverse.shape[0]
    position = lax.axis_index("row")
    first_rows = broadcast(test_kernel[:block], "row", 0)
    first_solved = product(first_inverse, first_rows)
    update_one = folding(first_solved, lax.all_gather(first_panel, "col", axis=1, tiled=True))
    partial_value = test_kernel - update_one
    second_rows = broadcast(partial_value[:block], "row", 1)
    second_solved = product(second_inverse, second_rows)
    update_two = folding(second_solved, lax.all_gather(second_panel, "col", axis=1, tiled=True))
    final = partial_value - update_two
    leading_final = jnp.where(
        position == 0, first_solved, jnp.where(position == 1, second_solved, final[:block])
    )
    return final.at[:block].set(leading_final)


def solution(mesh):
    in_specs = (P("row", "col"), P("row", "col"), P("row", "col"), P(), P())
    out_specs = P("row", "col")
    return jax.shard_map(
        per_device, mesh=mesh, in_specs=in_specs, out_specs=out_specs, check_vma=False
    )
```

profile of v0, /device:TPU:1, one launch (start us, length us, event | category | flops | bytes accessed | tf_op | source)
XLA Modules:
  0.0 296.1 jit_solution(15105920552222023866)
XLA Ops:
  7.4 0.0 copy-start
  7.4 0.0 all-reduce.3.cloned.1.call-start
  7.4 5.4 %copy.7 = f32[2048,512]{0,1:T(8,128)} copy(f32[2048,512]{1,0:T(8,128)} %param.7) | data formatting | bytes 8388608 | tf_op args[0]
  12.8 2.3 slice_select_fusion.2
  15.1 0.0 all-reduce.3.cloned.1.call-update
  15.1 0.0 all-gather.3.cloned.1.call-start
  15.2 0.5 all-gather.3.cloned.1.call-update
  15.7 0.0 all-reduce.5.cloned.1.call-start
  15.8 119.1 %all-reduce.3.cloned.1.call-done = f32[512,512]{0,1:T(8,128)} async-done(((f32[512,512]{0,1:T(8,128)}), f32[512,512]{0,1:T(8,128)}) %all-reduce.3.cloned.1.call-update) | async-done | bytes 1048592 | tf_op jit(solution)/shard_map/psum | solution.py:9
  134.9 0.0 copy-done
  134.9 3.1 %fusion.2 = f32[512,512]{1,0:T(8,128)S(1)} fusion(f32[512,512]{0,1:T(8,128)} %all-reduce.3.cloned.1.call-done, f32[512,512]{1,0:T(8,128)S(1)} %copy-done), kind=kOutput, calls=%fused_computation.7 | convolution fusion | flops 1610612736 | bytes 3145728 | tf_op jit(solution)/shard_map/dot_general | solution.py:13
  138.0 0.0 all-gather.3.cloned.1.call-done
  138.0 9.4 %bitcast_subtract_fusion.1 = f32[2048,512]{0,1:T(8,128)S(1)} fusion(f32[2048,512]{0,1:T(8,128)} %copy.7, f32[512,512]{1,0:T(8,128)S(1)} %fusion.2, f32[2048,512]{0,1:T(8,128)} %all-gather.3.cloned.1.call-done), kind=kOutput, calls=%fused_computation.1 | convolution fusion | flops 6443499520 | bytes 13631488 | tf_op jit(solution)/shard_map/dot_general | solution.py:13
  147.5 0.0 copy-start.1
  147.5 2.0 copy-done.1
  149.5 1.1 slice_select_fusion.1
  150.6 0.0 all-reduce.5.cloned.1.call-update
  150.6 0.2 all-gather.5.cloned.1.call-start
  150.9 0.4 all-gather.5.cloned.1.call-update
  151.2 115.2 %all-reduce.5.cloned.1.call-done = f32[512,512]{0,1:T(8,128)} async-done(((f32[512,512]{0,1:T(8,128)}), f32[512,512]{0,1:T(8,128)}) %all-reduce.5.cloned.1.call-update) | async-done | bytes 1048592 | tf_op jit(solution)/shard_map/psum | solution.py:9
  266.5 3.4 %fusion.3 = f32[512,512]{1,0:T(8,128)S(1)} fusion(f32[512,512]{0,1:T(8,128)} %all-reduce.5.cloned.1.call-done, f32[512,512]{1,0:T(8,128)} %param.11), kind=kOutput, calls=%fused_computation.8 | convolution fusion | flops 1610612736 | bytes 3145728 | tf_op jit(solution)/shard_map/dot_general | solution.py:13
  269.9 0.0 all-gather.5.cloned.1.call-done
  269.9 10.8 %bitcast_subtract_fusion = f32[2048,512]{0,1:T(8,128)} fusion(f32[2048,512]{0,1:T(8,128)} %copy-done.1, f32[512,512]{1,0:T(8,128)S(1)} %fusion.3, f32[2048,512]{0,1:T(8,128)} %all-gather.5.cloned.1.call-done), kind=kOutput, calls=%fused_computation | convolution fusion | flops 6443499520 | bytes 13631488 | tf_op jit(solution)/shard_map/dot_general | solution.py:13
  280.7 2.6 fusion.1
  283.3 5.3 %copy.8 = f32[2048,512]{1,0:T(8,128)} copy(f32[2048,512]{0,1:T(8,128)} %fusion.1) | data formatting | bytes 8388608 | tf_op jit(solution)/shard_map/scatter | solution.py:34
Async XLA Ops:
  7.4 127.6 %copy-start = (f32[512,512]{1,0:T(8,128)S(1)}, f32[512,512]{1,0:T(8,128)}, u32[]{:S(2)}) copy-start(f32[512,512]{1,0:T(8,128)} %param.10) | copy-start | bytes 3145732
  7.4 127.5 %all-reduce.3.cloned.1.call-start = ((), (), s32[]{:S(2)}) async-start(), calls=%async_computation | async-start | bytes 2097152 | tf_op jit(solution)/shard_map/psum | solution.py:9
  15.1 122.9 %all-gather.3.cloned.1.call-start = ((), (), s32[]{:S(2)}) async-start(), calls=%async_computation.1 | async-start | bytes 4718592 | tf_op jit(solution)/shard_map/all_gather | solution.py:25
  15.7 250.7 %all-reduce.5.cloned.1.call-start = ((), (), s32[]{:S(2)}) async-start(), calls=%async_computation.2 | async-start | bytes 2097152 | tf_op jit(solution)/shard_map/psum | solution.py:9
  147.5 2.0 copy-start.1
  150.6 119.3 %all-gather.5.cloned.1.call-start = ((), (), s32[]{:S(2)}) async-start(), calls=%async_computation.3 | async-start | bytes 4718592 | tf_op jit(solution)/shard_map/all_gather | solution.py:29
Sparse Core Ops, SparseCore 0:
  15.3 119.6 all-reduce.2
  150.8 115.6 all-reduce.4
Sparse Core Ops, SparseCore 1:
  17.5 58.4 all-gather.2
  152.9 54.4 all-gather.4
where the time goes:
time: 296 us
  waiting for transfers between devices  235 us (79%)
  matrix products  26.7 us (9%)
  between operations  14.9 us (5%)
  local copies, waits for them, and re-layouts  12.8 us (4%)
  other arithmetic  6.08 us (2%)
    psum x2, waiting for transfers between devices, broadcast(): return lax.psum(kept, axis)  234 us
    dot_general x4, matrix products, product(): jnp.dot(left, right, precision=lax.Precision.HIGHEST, preferred_element_t...  26.7 us
    unnamed x5, local copies, waits for them, and re-layouts  7.44 us
  transfers between devices with their start and end apart: 4, of which 2 were waited for; matrix products, arithmetic and copies ran while one was open for 2% of the time, Pallas kernels for 0%

commit v1 on v0

v1 whole, which is shorter than its diff:
```python
import jax
import jax.numpy as jnp
from jax import lax
from jax.experimental import pallas as pl
from jax.experimental.pallas import tpu as pltpu
from jax.sharding import PartitionSpec as P

MESH = pl.DeviceIdType.MESH
F32 = jnp.float32
BF16 = jnp.bfloat16
NX, NY = 4, 4
SIDES = (0, 1)


def split(value):
    high = value.astype(BF16)
    return high, (value - high.astype(F32)).astype(BF16)


def product(left, right_high, right_low):
    high, low = split(left)

    def dot(a, b):
        return jnp.dot(a, b, preferred_element_type=F32)

    return dot(high, right_high) + (dot(low, right_high) + dot(high, right_low))


def kernel(
    t_hbm, p1_hbm, p2_hbm, inv1, inv2, out_hbm,
    pg, pb, t1, t2, acc, s1, s2, sh, sl, rh, rl,
    zs, zr, xs, xr, local, tload, oload,
):
    nz = pg.shape[1]
    kc = pg.shape[2]
    half = nz // 2
    block = t1.shape[0]
    nblocks = acc.shape[0] // block
    npieces = 2 * nblocks
    xp = block // nz
    row = lax.axis_index("row")
    z = lax.axis_index("col")
    core = lax.rem(row, 2)
    y = lax.rem(row // 2, NY)
    x = row // (2 * NY)

    def at(xx, yy, cc):
        return (xx * NY + yy) * 2 + cc

    sibling = at(x, y, 1 - core)
    source = jnp.logical_and(x == 0, y == 0)
    other = jnp.logical_not(source)
    panels = (p1_hbm, p2_hbm)

    def origin(k):
        return lax.rem(z + (k + nz), nz)

    barrier = pltpu.get_barrier_semaphore()
    neighbours = (
        (row, origin(1)),
        (row, origin(-1)),
        (at(lax.rem(x + 1, NX), y, core), z),
        (at(lax.rem(x + NX - 1, NX), y, core), z),
        (at(x, lax.rem(y + 1, NY), core), z),
        (at(x, lax.rem(y + NY - 1, NY), core), z),
        (sibling, z),
    )

    def load_rows(b):
        part = pl.ds(b * block, block)
        return pltpu.make_async_copy(t_hbm.at[part], acc.at[part], tload.at[b])

    def own_panel(p):
        return pltpu.make_async_copy(panels[p], pg.at[p, z], local.at[p])

    for b in range(nblocks):
        load_rows(b).start()
    for p in range(2):
        own_panel(p).start()
    for n in neighbours:
        pl.semaphore_signal(barrier, inc=1, device_id=n, device_id_type=MESH)
    pl.semaphore_wait(barrier, len(neighbours))

    def where(j):
        return j // nblocks, pl.ds((j % nblocks) * block, block)

    def hops(side, j):
        return half if (j % 2 == side) else half - 1

    def zsend(side, h, j):
        if h > hops(side, j):
            return
        p, lanes = where(j)
        sign = -1 if side == 0 else 1
        owner = origin(sign * (h - 1))
        src = panels[p].at[:, lanes] if h == 1 else pg.at[p, owner, :, lanes]
        pltpu.make_async_remote_copy(
            src_ref=src,
            dst_ref=pg.at[p, owner, :, lanes],
            send_sem=zs.at[side, h - 1],
            recv_sem=zr.at[side, h - 1, j],
            device_id=(row, origin(-sign)),
            device_id_type=MESH,
        ).start()

    def zwait(side, h, j):
        if h > hops(side, j):
            return
        p, lanes = where(j)
        owner = origin(-h if side == 0 else h)
        ref = pg.at[p, owner, :, lanes]
        pltpu.make_async_remote_copy(
            src_ref=ref,
            dst_ref=ref,
            send_sem=zs.at[side, h - 1],
            recv_sem=zr.at[side, h - 1, j],
            device_id=(row, origin(1)),
            device_id_type=MESH,
        ).wait_recv()

    def first(j):
        for side in SIDES:
            zsend(side, 1, j)

    def forward(h, j):
        for side in SIDES:
            zwait(side, h, j)
            zsend(side, h + 1, j)

    buffers = (t1, t2, pb)
    order = [0]
    for d in range(1, half):
        order += [-d, d]
    order += [half]

    def piece(array, i):
        index = i if array < 2 else origin(order[i])
        return pl.ds(pl.multiple_of(index * xp, xp), xp)

    def xcopy(array, i, slot, src, target):
        return pltpu.make_async_remote_copy(
            src_ref=src,
            dst_ref=buffers[array].at[piece(array, i)],
            send_sem=xs.at[array, slot],
            recv_sem=xr.at[array, i],
            device_id=(target, z),
            device_id_type=MESH,
        )

    def to_children(array, i, src):
        @pl.when(jnp.logical_and(y == 0, x <= 1))
        def _():
            xcopy(array, i, 0, src, at(x + 1, y, core)).start()

        @pl.when(jnp.logical_and(y == 0, x == 0))
        def _():
            xcopy(array, i, 1, src, at(NX - 1, y, core)).start()

        @pl.when(y <= 1)
        def _():
            xcopy(array, i, 2, src, at(x, y + 1, core)).start()

        @pl.when(y == 0)
        def _():
            xcopy(array, i, 3, src, at(x, NY - 1, core)).start()

        xcopy(array, i, 4, src, sibling).start()

    def xwait(array, i):
        ref = buffers[array].at[piece(array, i)]
        xcopy(array, i, 4, ref, sibling).wait_recv()

    def xforward(array, i):
        xwait(array, i)

        @pl.when(core == min(array, 1))
        def _():
            to_children(array, i, buffers[array].at[piece(array, i)])

    def drain(array):
        whole = buffers[array]

        def wait(slot):
            pltpu.make_async_remote_copy(
                src_ref=whole, dst_ref=whole, send_sem=xs.at[array, slot], recv_sem=xr.at[array, 0],
                device_id=(sibling, z), device_id_type=MESH,
            ).wait_send()

        @pl.when(core == min(array, 1))
        def _():
            @pl.when(jnp.logical_and(y == 0, x <= 1))
            def _():
                wait(0)

            @pl.when(jnp.logical_and(y == 0, x == 0))
            def _():
                wait(1)

            @pl.when(y <= 1)
            def _():
                wait(2)

            @pl.when(y == 0)
            def _():
                wait(3)

            wait(4)

    def keep_rows(array):
        return pltpu.make_async_copy(t_hbm.at[pl.ds(0, block)], buffers[array], local.at[2])

    def keep_panel(i):
        return pltpu.make_async_copy(
            pg.at[0, origin(order[i]), :, pl.ds(0, block)], pb.at[piece(2, i)], local.at[3]
        )

    def panel_piece(i):
        src = pg.at[0, origin(order[i]), :, pl.ds(0, block)]

        @pl.when(core == 1)
        def _():
            to_children(2, i, src)
            keep_panel(i).start()

    @pl.when(source)
    def _():
        for array in range(2):
            @pl.when(core == array)
            def _():
                keep_rows(array).start()
                for i in range(nz):
                    to_children(array, i, t_hbm.at[pl.ds(i * xp, xp)])

        first(0)
        first(1)
        own_panel(0).wait()
        panel_piece(0)
        for h in range(1, half):
            forward(h, 0)
            first(h + 1)
            panel_piece(2 * h - 1)
            panel_piece(2 * h)
        for j in range(half + 1, npieces):
            first(j)
        zwait(0, half, 0)
        panel_piece(nz - 1)
        for array in range(2):
            @pl.when(core == array)
            def _():
                keep_rows(array).wait()

            @pl.when(core != array)
            def _():
                for i in range(nz):
                    xwait(array, i)
        for j in range(1, npieces):
            forward(1, j)

    @pl.when(other)
    def _():
        for j in range(npieces):
            first(j)
        own_panel(0).wait()
        for i in range(nz):
            xforward(0, i)
            xforward(1, i)
            if i < npieces:
                forward(1, i)

    own_panel(1).wait()

    tile = 256

    def solve(inverse, into):
        @pl.loop(0, block // tile)
        def _(i):
            rows = pl.ds(pl.multiple_of(i * tile, tile), tile)
            into[rows, :] = product(inverse[rows, :], rh[...], rl[...])

    def keep_split(p, value):
        high, low = split(value)
        sh[p] = high
        sl[p] = low

    rh[...], rl[...] = split(t1[...])
    solve(inv1, s1)
    keep_split(0, s1[...])

    @pl.when(source)
    def _():
        for j in range(1, npieces):
            forward(2, j)

        @pl.when(core == 1)
        def _():
            whole = pltpu.make_async_copy(pb, pb, local.at[3])
            whole.wait()

        @pl.when(core == 0)
        def _():
            for i in range(nz):
                xwait(2, i)

    @pl.when(other)
    def _():
        for i in range(nz):
            xforward(2, i)
            if i < npieces:
                forward(2, i)

    @pl.loop(0, block // tile)
    def _(i):
        lanes = pl.ds(pl.multiple_of(i * tile, tile), tile)
        value = t2[lanes, :] - product(pb[:, lanes].T, sh[0], sl[0])
        rh[lanes, :], rl[lanes, :] = split(value)

    solve(inv2, s2)
    keep_split(1, s2[...])

    for b in range(nblocks):
        load_rows(b).wait()

    def update(b, origins):
        ks = [pl.ds(pl.multiple_of(o * kc, kc), kc) for o in origins]
        right_high = jnp.concatenate([sh[p, k, :] for k in ks for p in range(2)], axis=0)
        right_low = jnp.concatenate([sl[p, k, :] for k in ks for p in range(2)], axis=0)

        @pl.loop(0, block // tile)
        def _(i):
            rows = pl.ds(pl.multiple_of(b * block + i * tile, tile), tile)
            left = jnp.concatenate([pg[p, o, :, rows] for o in origins for p in range(2)], axis=0)
            acc[rows, :] = acc[rows, :] - product(left.T, right_high, right_low)

    units = [(b, d) for d in (1, 2) for b in range(nblocks)]
    for j in range(npieces):
        if j == 0:
            @pl.when(other)
            def _():
                forward(half - 1, 0)
        else:
            forward(half - 1, j)
        if j < len(units):
            b, d = units[j]
            update(b, (origin(-d), origin(d)))
    for b in range(nblocks):
        update(b, (origin(-3), origin(3)))
    for b in range(nblocks):
        update(b, (z,))

    def store_rows(b):
        part = pl.ds(b * block, block)
        return pltpu.make_async_copy(acc.at[part], out_hbm.at[part], oload.at[b])

    for b in range(nblocks):
        for j in (b, b + nblocks):
            for side in SIDES:
                if j == 0:
                    @pl.when(other)
                    def _():
                        zwait(side, half, 0)
                else:
                    zwait(side, half, j)
        update(b, (origin(half),))
        if b == 0:
            @pl.when(row == 0)
            def _():
                acc[pl.ds(0, block), :] = s1[...]

            @pl.when(row == 1)
            def _():
                acc[pl.ds(0, block), :] = s2[...]
        store_rows(b).start()

    for side in SIDES:
        for h in range(1, half + 1):
            ref = pg.at[:, z] if h < half else pg.at[0, z]
            pltpu.make_async_remote_copy(
                src_ref=ref, dst_ref=ref, send_sem=zs.at[side, h - 1], recv_sem=zr.at[side, h - 1, 0],
                device_id=(row, origin(1)), device_id_type=MESH,
            ).wait_send()
    for array in range(3):
        drain(array)
    for b in range(nblocks):
        store_rows(b).wait()


def per_device(nz, test_kernel, first_panel, second_panel, first_inverse, second_inverse):
    rows, cols = test_kernel.shape
    kc = first_panel.shape[1]
    block = first_inverse.shape[0]
    vmem = pl.BlockSpec(memory_space=pltpu.VMEM)
    hbm = pl.BlockSpec(memory_space=pl.ANY)
    dma = pltpu.SemaphoreType.DMA
    nblocks = rows // block
    return pl.pallas_call(
        kernel,
        out_shape=jax.ShapeDtypeStruct((rows, cols), F32),
        in_specs=[hbm, hbm, hbm, vmem, vmem],
        out_specs=hbm,
        scratch_shapes=[
            pltpu.VMEM((2, nz, kc, rows), F32),
            pltpu.VMEM((block, block), F32),
            pltpu.VMEM((block, cols), F32),
            pltpu.VMEM((block, cols), F32),
            pltpu.VMEM((rows, cols), F32),
            pltpu.VMEM((block, cols), F32),
            pltpu.VMEM((block, cols), F32),
            pltpu.VMEM((2, block, cols), BF16),
            pltpu.VMEM((2, block, cols), BF16),
            pltpu.VMEM((block, cols), BF16),
            pltpu.VMEM((block, cols), BF16),
            dma((2, nz // 2)),
            dma((2, nz // 2, 2 * nblocks)),
            dma((3, 5)),
            dma((3, nz)),
            dma((4,)),
            dma((nblocks,)),
            dma((nblocks,)),
        ],
        compiler_params=pltpu.CompilerParams(
            collective_id=0, has_side_effects=True, vmem_limit_bytes=40 * 1024 * 1024
        ),
    )(test_kernel, first_panel.T, second_panel.T, first_inverse, second_inverse)


def solution(mesh):
    nz = mesh.shape["col"]

    def run(*args):
        return per_device(nz, *args)

    in_specs = (P("row", "col"), P("row", "col"), P("row", "col"), P(), P())
    return jax.shard_map(run, mesh=mesh, in_specs=in_specs, out_specs=P("row", "col"), check_vma=False)
```

time: 296 us -> 102 us (0.34)
  waiting for transfers between devices: 235 us -> 0 us
  Pallas kernels: 0 us -> 92.5 us
  matrix products: 26.7 us -> 0 us
  between operations: 14.9 us -> 0.01 us
  other arithmetic: 6.08 us -> 0 us
  local copies, waits for them, and re-layouts: 12.8 us -> 8.73 us
    psum x2 -> x0, waiting for transfers between devices: 234 us -> none  [broadcast(): return lax.psum(kept, axis)]
    pallas_call x0 -> x1, Pallas kernels: none -> 92.5 us  [per_device(): pl.pallas_call(kernel, out_shape=jax.ShapeDtypeStruct((rows, cols), F32),...]
    dot_general x4 -> x0, matrix products: 26.7 us -> none  [product(): jnp.dot(left, right, precision=lax.Precision.HIGHEST, preferred_element_t...]
    scatter x1 -> x0, local copies, waits for them, and re-layouts: 5.34 us -> none  [per_device(): return final.at[:block].set(leading_final)]
    select_n x2 -> x0, other arithmetic: 3.46 us -> none  [broadcast(): jnp.where(lax.axis_index(axis) == source, value, 0).astype(value.dtype)]
    unnamed x5 -> x11, local copies, waits for them, and re-layouts: 7.44 us -> 8.73 us
  transfers between devices with their start and end apart: 4 -> 0, of which waited for: 2 -> 0; matrix products, arithmetic and copies ran while one was open for 2% -> 0% of each run, Pallas kernels for 0% -> 0%
where the time goes in v1:
time: 102 us; the launch traced here: 101 us
  Pallas kernels  92.5 us (91%)
  local copies, waits for them, and re-layouts  8.73 us (9%)
    pallas_call x1, Pallas kernels, per_device(): pl.pallas_call(kernel, out_shape=jax.ShapeDtypeStruct((rows, cols), F32),...  92.5 us
    unnamed x11, local copies, waits for them, and re-layouts  8.73 us

profile of v1, /device:TPU:1, one launch (start us, length us, event | category | flops | bytes accessed | tf_op | source)
XLA Modules:
  0.0 101.3 jit_solution(9172209491077101398)
XLA Ops:
  0.0 0.0 copy-start
  0.0 2.2 %copy-done = f32[2048,512]{1,0:T(8,128)S(1)} copy-done((f32[2048,512]{1,0:T(8,128)S(1)}, f32[2048,512]{1,0:T(8,128)}, u32[]{:S(2)}) %copy-start) | copy-done | bytes 4194328
  2.2 0.0 copy-start.1
  2.2 1.2 %copy-done.1 = f32[512,512]{1,0:T(8,128)S(1)} copy-done((f32[512,512]{1,0:T(8,128)S(1)}, f32[512,512]{1,0:T(8,128)}, u32[]{:S(2)}) %copy-start.1) | copy-done | bytes 1048600
  3.4 0.0 copy-start.2
  3.4 1.2 %copy-done.2 = f32[512,512]{1,0:T(8,128)S(1)} copy-done((f32[512,512]{1,0:T(8,128)S(1)}, f32[512,512]{1,0:T(8,128)}, u32[]{:S(2)}) %copy-start.2) | copy-done | bytes 1048600
  4.6 0.0 copy-start.3
  4.6 1.0 %copy-done.3 = f32[2048,64]{0,1:T(8,128)S(1)} copy-done((f32[2048,64]{0,1:T(8,128)S(1)}, f32[2048,64]{0,1:T(8,128)}, u32[]{:S(2)}) %copy-start.3) | copy-done | bytes 524312
  5.7 0.0 copy-start.4
  5.7 1.0 %copy-done.4 = f32[2048,64]{0,1:T(8,128)S(1)} copy-done((f32[2048,64]{0,1:T(8,128)S(1)}, f32[2048,64]{0,1:T(8,128)}, u32[]{:S(2)}) %copy-start.4) | copy-done | bytes 524312
  6.7 92.5 %shard_map.55 = f32[2048,512]{1,0:T(8,128)S(1)} custom-call(f32[2048,512]{1,0:T(8,128)S(1)} %copy-done, f32[64,2048]{1,0:T(8,128)S(1)} %bitcast.2, f32[64,2048]{1,0:T(8,128)S(1)} %bitcast.3, f32[512,512]{1,0:T(8,128)S(1)} %copy-done.1, f32[512,512]{1,0:T(8,128)S(1)} %copy-done.2), custom_call_target="tpu_custom_call" | custom-call | tf_op jit(solution)/shard_map/pallas_call | solution.py:395
  99.3 2.0 %copy.7 = f32[2048,512]{1,0:T(8,128)} copy(f32[2048,512]{1,0:T(8,128)S(1)} %shard_map.55) | data formatting | bytes 8388608
Async XLA Ops:
  0.0 2.2 %copy-start = (f32[2048,512]{1,0:T(8,128)S(1)}, f32[2048,512]{1,0:T(8,128)}, u32[]{:S(2)}) copy-start(f32[2048,512]{1,0:T(8,128)} %t_hbm.1) | copy-start | bytes 12582916
  2.2 1.2 %copy-start.1 = (f32[512,512]{1,0:T(8,128)S(1)}, f32[512,512]{1,0:T(8,128)}, u32[]{:S(2)}) copy-start(f32[512,512]{1,0:T(8,128)} %inv1.1) | copy-start | bytes 3145732
  3.4 1.2 %copy-start.2 = (f32[512,512]{1,0:T(8,128)S(1)}, f32[512,512]{1,0:T(8,128)}, u32[]{:S(2)}) copy-start(f32[512,512]{1,0:T(8,128)} %inv2.1) | copy-start | bytes 3145732
  4.6 1.0 %copy-start.3 = (f32[2048,64]{0,1:T(8,128)S(1)}, f32[2048,64]{0,1:T(8,128)}, u32[]{:S(2)}) copy-start(f32[2048,64]{0,1:T(8,128)} %param.6) | copy-start | bytes 1572868
  5.7 1.0 %copy-start.4 = (f32[2048,64]{0,1:T(8,128)S(1)}, f32[2048,64]{0,1:T(8,128)}, u32[]{:S(2)}) copy-start(f32[2048,64]{0,1:T(8,128)} %param.7) | copy-start | bytes 1572868

commit v2 on v1

--- a/solution.py
+++ b/solution.py
@@ -1,3 +1,5 @@
+import functools
+
 import jax
 import jax.numpy as jnp
 from jax import lax
@@ -10,6 +12,8 @@
 BF16 = jnp.bfloat16
 NX, NY = 4, 4
 SIDES = (0, 1)
+VMEM_BYTES = 60 * 1024 * 1024
+CHUNKS = 4
 
 
 def split(value):
@@ -17,18 +21,27 @@
     return high, (value - high.astype(F32)).astype(BF16)
 
 
+def dot(left, right):
+    return jnp.dot(left, right, preferred_element_type=F32)
+
+
 def product(left, right_high, right_low):
     high, low = split(left)
-
-    def dot(a, b):
-        return jnp.dot(a, b, preferred_element_type=F32)
-
     return dot(high, right_high) + (dot(low, right_high) + dot(high, right_low))
 
 
+def turned_product(left, right_high, right_low):
+    high, low = split(left)
+    high, low = high.T, low.T
+    return dot(
+        jnp.concatenate([high, low, high], axis=1),
+        jnp.concatenate([right_high, right_high, right_low], axis=0),
+    )
+
+
 def kernel(
-    t_hbm, p1_hbm, p2_hbm, inv1, inv2, out_hbm,
-    pg, pb, t1, t2, acc, s1, s2, sh, sl, rh, rl,
+    t_hbm, p1_hbm, p2_hbm, inv1, inv2, acc_hbm, last_hbm, right_hbm,
+    pg, pb, t1, t2, acc, s1, s2, sh, sl, rh, rl, right,
     zs, zr, xs, xr, local, tload, oload,
 ):
     nz = pg.shape[1]
@@ -94,9 +107,10 @@
         sign = -1 if side == 0 else 1
         owner = origin(sign * (h - 1))
         src = panels[p].at[:, lanes] if h == 1 else pg.at[p, owner, :, lanes]
+        dst = last_hbm.at[p, :, lanes] if h == half else pg.at[p, owner, :, lanes]
         pltpu.make_async_remote_copy(
             src_ref=src,
-            dst_ref=pg.at[p, owner, :, lanes],
+            dst_ref=dst,
             send_sem=zs.at[side, h - 1],
             recv_sem=zr.at[side, h - 1, j],
             device_id=(row, origin(-sign)),
@@ -108,7 +122,7 @@
             return
         p, lanes = where(j)
         owner = origin(-h if side == 0 else h)
-        ref = pg.at[p, owner, :, lanes]
+        ref = last_hbm.at[p, :, lanes] if h == half else pg.at[p, owner, :, lanes]
         pltpu.make_async_remote_copy(
             src_ref=ref,
             dst_ref=ref,
@@ -141,28 +155,30 @@
         return pltpu.make_async_remote_copy(
             src_ref=src,
             dst_ref=buffers[array].at[piece(array, i)],
-            send_sem=xs.at[array, slot],
+            send_sem=xs.at[array, i % 2, slot],
             recv_sem=xr.at[array, i],
             device_id=(target, z),
             device_id_type=MESH,
         )
 
+    def edges(tree):
+        u, v = x, y
+
+        def to(uu, vv):
+            return at(uu, vv, core)
+
+        return (
+            (jnp.logical_and(v == 0, u <= 1), to(lax.rem(u + 1, NX), v)),
+            (jnp.logical_and(v == 0, u == 0), to(NX - 1, v)),
+            (v <= 1, to(u, lax.rem(v + 1, NX))),
+            (v == 0, to(u, NX - 1)),
+        )
+
     def to_children(array, i, src):
-        @pl.when(jnp.logical_and(y == 0, x <= 1))
-        def _():
-            xcopy(array, i, 0, src, at(x + 1, y, core)).start()
-
-        @pl.when(jnp.logical_and(y == 0, x == 0))
-        def _():
-            xcopy(array, i, 1, src, at(NX - 1, y, core)).start()
-
-        @pl.when(y <= 1)
-        def _():
-            xcopy(array, i, 2, src, at(x, y + 1, core)).start()
-
-        @pl.when(y == 0)
-        def _():
-            xcopy(array, i, 3, src, at(x, NY - 1, core)).start()
+        for slot, (sends, target) in enumerate(edges(i % 2)):
+            @pl.when(sends)
+            def _():
+                xcopy(array, i, slot, src, target).start()
 
         xcopy(array, i, 4, src, sibling).start()
 
@@ -178,44 +194,38 @@
             to_children(array, i, buffers[array].at[piece(array, i)])
 
     def drain(array):
-        whole = buffers[array]
-
-        def wait(slot):
+        pieces = buffers[array].at[pl.ds(0, block // 2)]
+
+        def wait(tree, slot):
             pltpu.make_async_remote_copy(
-                src_ref=whole, dst_ref=whole, send_sem=xs.at[array, slot], recv_sem=xr.at[array, 0],
+                src_ref=pieces, dst_ref=pieces, send_sem=xs.at[array, tree, slot], recv_sem=xr.at[array, 0],
                 device_id=(sibling, z), device_id_type=MESH,
             ).wait_send()
 
         @pl.when(core == min(array, 1))
         def _():
-            @pl.when(jnp.logical_and(y == 0, x <= 1))
-            def _():
-                wait(0)
-
-            @pl.when(jnp.logical_and(y == 0, x == 0))
-            def _():
-                wait(1)
-
-            @pl.when(y <= 1)
-            def _():
-                wait(2)
-
-            @pl.when(y == 0)
-            def _():
-                wait(3)
-
-            wait(4)
+            for tree in range(2):
+                for slot, (sends, _unused) in enumerate(edges(tree)):
+                    @pl.when(sends)
+                    def _():
+                        wait(tree, slot)
+
+                wait(tree, 4)
 
     def keep_rows(array):
         return pltpu.make_async_copy(t_hbm.at[pl.ds(0, block)], buffers[array], local.at[2])
 
+    def held_piece(i):
+        lanes = pl.ds(0, block)
+        if order[i] == half:
+            return last_hbm.at[0, :, lanes]
+        return pg.at[0, origin(order[i]), :, lanes]
+
     def keep_panel(i):
-        return pltpu.make_async_copy(
-            pg.at[0, origin(order[i]), :, pl.ds(0, block)], pb.at[piece(2, i)], local.at[3]
-        )
+        return pltpu.make_async_copy(held_piece(i), pb.at[piece(2, i)], local.at[3])
 
     def panel_piece(i):
-        src = pg.at[0, origin(order[i]), :, pl.ds(0, block)]
+        src = held_piece(i)
 
         @pl.when(core == 1)
         def _():
@@ -269,32 +279,23 @@
 
     own_panel(1).wait()
 
-    tile = 256
-
-    def solve(inverse, into):
-        @pl.loop(0, block // tile)
-        def _(i):
-            rows = pl.ds(pl.multiple_of(i * tile, tile), tile)
-            into[rows, :] = product(inverse[rows, :], rh[...], rl[...])
-
     def keep_split(p, value):
         high, low = split(value)
         sh[p] = high
         sl[p] = low
 
     rh[...], rl[...] = split(t1[...])
-    solve(inv1, s1)
+    s1[...] = product(inv1[...], rh[...], rl[...])
     keep_split(0, s1[...])
 
     @pl.when(source)
     def _():
-        for j in range(1, npieces):
+        for j in range(1, nblocks):
             forward(2, j)
 
         @pl.when(core == 1)
         def _():
-            whole = pltpu.make_async_copy(pb, pb, local.at[3])
-            whole.wait()
+            pltpu.make_async_copy(pb, pb, local.at[3]).wait()
 
         @pl.when(core == 0)
         def _():
@@ -305,33 +306,33 @@
     def _():
         for i in range(nz):
             xforward(2, i)
-            if i < npieces:
-                forward(2, i)
-
-    @pl.loop(0, block // tile)
-    def _(i):
-        lanes = pl.ds(pl.multiple_of(i * tile, tile), tile)
-        value = t2[lanes, :] - product(pb[:, lanes].T, sh[0], sl[0])
-        rh[lanes, :], rl[lanes, :] = split(value)
-
-    solve(inv2, s2)
+            if i >= half:
+                forward(2, i - half)
+
+    rh[...], rl[...] = split(t2[...] - turned_product(pb[...], sh[0], sl[0]))
+    s2[...] = product(inv2[...], rh[...], rl[...])
     keep_split(1, s2[...])
-
-    for b in range(nblocks):
-        load_rows(b).wait()
 
     def update(b, origins):
         ks = [pl.ds(pl.multiple_of(o * kc, kc), kc) for o in origins]
-        right_high = jnp.concatenate([sh[p, k, :] for k in ks for p in range(2)], axis=0)
-        right_low = jnp.concatenate([sl[p, k, :] for k in ks for p in range(2)], axis=0)
-
-        @pl.loop(0, block // tile)
-        def _(i):
-            rows = pl.ds(pl.multiple_of(b * block + i * tile, tile), tile)
-            left = jnp.concatenate([pg[p, o, :, rows] for o in origins for p in range(2)], axis=0)
-            acc[rows, :] = acc[rows, :] - product(left.T, right_high, right_low)
-
-    units = [(b, d) for d in (1, 2) for b in range(nblocks)]
+        rows = pl.ds(b * block, block)
+        acc[rows, :] = acc[rows, :] - turned_product(
+            jnp.concatenate([pg[p, o, :, rows] for o in origins for p in range(2)], axis=0),
+            jnp.concatenate([sh[p, k, :] for k in ks for p in range(2)], axis=0),
+            jnp.concatenate([sl[p, k, :] for k in ks for p in range(2)], axis=0),
+        )
+
+    near = (z, origin(-1), origin(1))
+    far = (origin(-2), origin(2), origin(-3), origin(3))
+    for b in range(nblocks):
+        forward(2, nblocks + b)
+        load_rows(b).wait()
+        update(b, near)
+
+    def store_rows(b):
+        part = pl.ds(b * block, block)
+        return pltpu.make_async_copy(acc.at[part], acc_hbm.at[part], oload.at[b])
+
     for j in range(npieces):
         if j == 0:
             @pl.when(other)
@@ -339,37 +340,33 @@
                 forward(half - 1, 0)
         else:
             forward(half - 1, j)
-        if j < len(units):
-            b, d = units[j]
-            update(b, (origin(-d), origin(d)))
-    for b in range(nblocks):
-        update(b, (origin(-3), origin(3)))
-    for b in range(nblocks):
-        update(b, (z,))
-
-    def store_rows(b):
-        part = pl.ds(b * block, block)
-        return pltpu.make_async_copy(acc.at[part], out_hbm.at[part], oload.at[b])
-
-    for b in range(nblocks):
-        for j in (b, b + nblocks):
-            for side in SIDES:
-                if j == 0:
-                    @pl.when(other)
-                    def _():
-                        zwait(side, half, 0)
-                else:
-                    zwait(side, half, j)
-        update(b, (origin(half),))
-        if b == 0:
-            @pl.when(row == 0)
-            def _():
-                acc[pl.ds(0, block), :] = s1[...]
-
-            @pl.when(row == 1)
-            def _():
-                acc[pl.ds(0, block), :] = s2[...]
-        store_rows(b).start()
+        if j >= nblocks:
+            b = j - nblocks
+            update(b, far)
+            if b == 0:
+                @pl.when(row == 0)
+                def _():
+                    acc[pl.ds(0, block), :] = s1[...]
+
+                @pl.when(row == 1)
+                def _():
+                    acc[pl.ds(0, block), :] = s2[...]
+            store_rows(b).start()
+
+    final = pl.ds(pl.multiple_of(origin(half) * kc, kc), kc)
+    for p in range(2):
+        right[0, pl.ds(p * kc, kc), :] = sh[p, final, :]
+        right[1, pl.ds(p * kc, kc), :] = sl[p, final, :]
+    store_right = pltpu.make_async_copy(right, right_hbm, local.at[2])
+    store_right.start()
+    for j in range(npieces):
+        for side in SIDES:
+            if j == 0:
+                @pl.when(other)
+                def _():
+                    zwait(side, half, 0)
+            else:
+                zwait(side, half, j)
 
     for side in SIDES:
         for h in range(1, half + 1):
@@ -380,8 +377,45 @@
             ).wait_send()
     for array in range(3):
         drain(array)
+    store_right.wait()
     for b in range(nblocks):
         store_rows(b).wait()
+
+
+def finish(block, acc_hbm, last_hbm, right_hbm, out_hbm, acc, last, right, sems):
+    tile = acc.shape[0] // CHUNKS
+    first_block = jnp.logical_not(lax.axis_index("row") < 2)
+    loads, stores = [], []
+    load_right = pltpu.make_async_copy(right_hbm, right, sems.at[3, 0])
+    load_right.start()
+    for i in range(CHUNKS):
+        part = pl.ds(i * tile, tile)
+        loads.append(
+            (
+                pltpu.make_async_copy(last_hbm.at[:, :, part], last.at[:, :, part], sems.at[0, i]),
+                pltpu.make_async_copy(acc_hbm.at[part], acc.at[part], sems.at[1, i]),
+            )
+        )
+        stores.append(pltpu.make_async_copy(acc.at[part], out_hbm.at[part], sems.at[2, i]))
+        for copy in loads[-1]:
+            copy.start()
+    load_right.wait()
+    for i in range(CHUNKS):
+        part = pl.ds(i * tile, tile)
+        for copy in loads[i]:
+            copy.wait()
+
+        def change():
+            left = jnp.concatenate([last[p, :, part] for p in range(2)], axis=0)
+            acc[part, :] = acc[part, :] - turned_product(left, right[0], right[1])
+
+        if i * tile < block:
+            pl.when(first_block)(change)
+        else:
+            change()
+        stores[i].start()
+    for copy in stores:
+        copy.wait()
 
 
 def per_device(nz, test_kernel, first_panel, second_panel, first_inverse, second_inverse):
@@ -392,11 +426,15 @@
     hbm = pl.BlockSpec(memory_space=pl.ANY)
     dma = pltpu.SemaphoreType.DMA
     nblocks = rows // block
-    return pl.pallas_call(
+    acc, last, right = pl.pallas_call(
         kernel,
-        out_shape=jax.ShapeDtypeStruct((rows, cols), F32),
+        out_shape=[
+            jax.ShapeDtypeStruct((rows, cols), F32),
+            jax.ShapeDtypeStruct((2, kc, rows), F32),
+            jax.ShapeDtypeStruct((2, 2 * kc, cols), BF16),
+        ],
         in_specs=[hbm, hbm, hbm, vmem, vmem],
-        out_specs=hbm,
+        out_specs=[hbm, hbm, hbm],
         scratch_shapes=[
             pltpu.VMEM((2, nz, kc, rows), F32),
             pltpu.VMEM((block, block), F32),
@@ -409,18 +447,32 @@
             pltpu.VMEM((2, block, cols), BF16),
             pltpu.VMEM((block, cols), BF16),
             pltpu.VMEM((block, cols), BF16),
+            pltpu.VMEM((2, 2 * kc, cols), BF16),
             dma((2, nz // 2)),
             dma((2, nz // 2, 2 * nblocks)),
-            dma((3, 5)),
+            dma((3, 2, 5)),
             dma((3, nz)),
             dma((4,)),
             dma((nblocks,)),
             dma((nblocks,)),
         ],
         compiler_params=pltpu.CompilerParams(
-            collective_id=0, has_side_effects=True, vmem_limit_bytes=40 * 1024 * 1024
+            collective_id=0, has_side_effects=True, vmem_limit_bytes=VMEM_BYTES
         ),
     )(test_kernel, first_panel.T, second_panel.T, first_inverse, second_inverse)
+    return pl.pallas_call(
+        functools.partial(finish, block),
+        out_shape=jax.ShapeDtypeStruct((rows, cols), F32),
+        in_specs=[hbm, hbm, hbm],
+        out_specs=hbm,
+        scratch_shapes=[
+            pltpu.VMEM((rows, cols), F32),
+            pltpu.VMEM((2, kc, rows), F32),
+            pltpu.VMEM((2, 2 * kc, cols), BF16),
+            dma((4, CHUNKS)),
+        ],
+        compiler_params=pltpu.CompilerParams(vmem_limit_bytes=VMEM_BYTES),
+    )(acc, last, right)
 
 
 def solution(mesh):

time: 102 us -> 96 us (0.941)
  local copies, waits for them, and re-layouts: 8.73 us -> 0 us
  Pallas kernels: 92.5 us -> 95.7 us
    unnamed x11 -> x0, local copies, waits for them, and re-layouts: 8.73 us -> none
    pallas_call x1 -> x2, Pallas kernels: 92.5 us -> 95.7 us  [the longest x1 91.2 us: per_device(): pl.pallas_call(kernel, out_shape=[jax.ShapeDtypeStruct((rows, cols), F32)...]
where the time goes in v2:
time: 96 us; the launch traced here: 95.7 us
  Pallas kernels  95.7 us (100%)
    pallas_call x1, Pallas kernels, per_device(): pl.pallas_call(kernel, out_shape=[jax.ShapeDtypeStruct((rows, cols), F32)...  91.2 us
    pallas_call x1, Pallas kernels, per_device(): pl.pallas_call(functools.partial(finish, block), out_shape=jax.ShapeDtype...  4.54 us

profile of v2, /device:TPU:1, one launch (start us, length us, event | category | flops | bytes accessed | tf_op | source)
XLA Modules:
  0.0 95.7 jit_solution(7444943314619598309)
XLA Ops:
  0.0 91.2 %shard_map.55 = (f32[2048,512]{1,0:T(8,128)}, f32[2,64,2048]{2,1,0:T(8,128)}, bf16[2,128,512]{2,1,0:T(8,128)(2,1)}) custom-call(f32[2048,512]{1,0:T(8,128)} %t_hbm.1, f32[64,2048]{1,0:T(8,128)} %bitcast.2, f32[64,2048]{1,0:T(8,128)} %bitcast.3, f32[512,512]{1,0:T(8,128)} %inv1.1, f32[512,512]{1,0:T(8,128)} %inv2.1), custom_call_target="tpu_custom_call" | custom-call | tf_op jit(solution)/shard_map/pallas_call | solution.py:429
  91.2 4.5 %shard_map.56 = f32[2048,512]{1,0:T(8,128)} custom-call(f32[2048,512]{1,0:T(8,128)} %get-tuple-element.8.acc_hbm, f32[2,64,2048]{2,1,0:T(8,128)} %get-tuple-element.9.last_hbm, bf16[2,128,512]{2,1,0:T(8,128)(2,1)} %get-tuple-element.10.right_hbm), custom_call_target="tpu_custom_call" | custom-call | tf_op jit(solution)/shard_map/pallas_call | solution.py:463

commit v3 on v2

--- a/solution.py
+++ b/solution.py
@@ -12,7 +12,9 @@
 BF16 = jnp.bfloat16
 NX, NY = 4, 4
 SIDES = (0, 1)
-VMEM_BYTES = 60 * 1024 * 1024
+VMEM_BYTES = 36 * 1024 * 1024
+FINISH_BYTES = 12 * 1024 * 1024
+EARLY = 2
 CHUNKS = 4
 
 
@@ -39,10 +41,22 @@
     )
 
 
+def finish_block(part, first, out, acc, last, right):
+
+    def change():
+        left = jnp.concatenate([last[p, :, part] for p in range(2)], axis=0)
+        out[part, :] = acc[part, :] - turned_product(left, right[0], right[1])
+
+    if first:
+        pl.when(lax.axis_index("row") >= 2)(change)
+    else:
+        change()
+
+
 def kernel(
-    t_hbm, p1_hbm, p2_hbm, inv1, inv2, acc_hbm, last_hbm, right_hbm,
-    pg, pb, t1, t2, acc, s1, s2, sh, sl, rh, rl, right,
-    zs, zr, xs, xr, local, tload, oload,
+    t_hbm, p1_hbm, p2_hbm, inv1_hbm, inv2_hbm, acc, last, right,
+    pg, pb, t1, t2, inv1, inv2, s1, s2, sh, sl, rh, rl,
+    zs, zr, xs, xr, local, tload,
 ):
     nz = pg.shape[1]
     kc = pg.shape[2]
@@ -86,8 +100,11 @@
     def own_panel(p):
         return pltpu.make_async_copy(panels[p], pg.at[p, z], local.at[p])
 
-    for b in range(nblocks):
-        load_rows(b).start()
+    inverses = ((inv1_hbm, inv1), (inv2_hbm, inv2))
+
+    def load_inverse(p):
+        return pltpu.make_async_copy(*inverses[p], local.at[4 + p])
+
     for p in range(2):
         own_panel(p).start()
     for n in neighbours:
@@ -107,7 +124,7 @@
         sign = -1 if side == 0 else 1
         owner = origin(sign * (h - 1))
         src = panels[p].at[:, lanes] if h == 1 else pg.at[p, owner, :, lanes]
-        dst = last_hbm.at[p, :, lanes] if h == half else pg.at[p, owner, :, lanes]
+        dst = last.at[p, :, lanes] if h == half else pg.at[p, owner, :, lanes]
         pltpu.make_async_remote_copy(
             src_ref=src,
             dst_ref=dst,
@@ -122,7 +139,7 @@
             return
         p, lanes = where(j)
         owner = origin(-h if side == 0 else h)
-        ref = last_hbm.at[p, :, lanes] if h == half else pg.at[p, owner, :, lanes]
+        ref = last.at[p, :, lanes] if h == half else pg.at[p, owner, :, lanes]
         pltpu.make_async_remote_copy(
             src_ref=ref,
             dst_ref=ref,
@@ -218,7 +235,7 @@
     def held_piece(i):
         lanes = pl.ds(0, block)
         if order[i] == half:
-            return last_hbm.at[0, :, lanes]
+            return last.at[0, :, lanes]
         return pg.at[0, origin(order[i]), :, lanes]
 
     def keep_panel(i):
@@ -231,6 +248,12 @@
         def _():
             to_children(2, i, src)
             keep_panel(i).start()
+
+    def start_loads():
+        for p in range(2):
+            load_inverse(p).start()
+        for b in range(nblocks):
+            load_rows(b).start()
 
     @pl.when(source)
     def _():
@@ -243,6 +266,7 @@
 
         first(0)
         first(1)
+        start_loads()
         own_panel(0).wait()
         panel_piece(0)
         for h in range(1, half):
@@ -270,6 +294,7 @@
     def _():
         for j in range(npieces):
             first(j)
+        start_loads()
         own_panel(0).wait()
         for i in range(nz):
             xforward(0, i)
@@ -285,6 +310,7 @@
         sl[p] = low
 
     rh[...], rl[...] = split(t1[...])
+    load_inverse(0).wait()
     s1[...] = product(inv1[...], rh[...], rl[...])
     keep_split(0, s1[...])
 
@@ -310,6 +336,7 @@
                 forward(2, i - half)
 
     rh[...], rl[...] = split(t2[...] - turned_product(pb[...], sh[0], sl[0]))
+    load_inverse(1).wait()
     s2[...] = product(inv2[...], rh[...], rl[...])
     keep_split(1, s2[...])
 
@@ -328,10 +355,6 @@
         forward(2, nblocks + b)
         load_rows(b).wait()
         update(b, near)
-
-    def store_rows(b):
-        part = pl.ds(b * block, block)
-        return pltpu.make_async_copy(acc.at[part], acc_hbm.at[part], oload.at[b])
 
     for j in range(npieces):
         if j == 0:
@@ -351,22 +374,22 @@
                 @pl.when(row == 1)
                 def _():
                     acc[pl.ds(0, block), :] = s2[...]
-            store_rows(b).start()
 
     final = pl.ds(pl.multiple_of(origin(half) * kc, kc), kc)
     for p in range(2):
         right[0, pl.ds(p * kc, kc), :] = sh[p, final, :]
         right[1, pl.ds(p * kc, kc), :] = sl[p, final, :]
-    store_right = pltpu.make_async_copy(right, right_hbm, local.at[2])
-    store_right.start()
-    for j in range(npieces):
-        for side in SIDES:
-            if j == 0:
-                @pl.when(other)
-                def _():
-                    zwait(side, half, 0)
-            else:
-                zwait(side, half, j)
+    for b in range(nblocks):
+        for j in (b, b + nblocks):
+            for side in SIDES:
+                if j == 0:
+                    @pl.when(other)
+                    def _():
+                        zwait(side, half, 0)
+                else:
+                    zwait(side, half, j)
+        if b < EARLY:
+            finish_block(pl.ds(b * block, block), b == 0, acc, acc, last, right)
 
     for side in SIDES:
         for h in range(1, half + 1):
@@ -377,43 +400,22 @@
             ).wait_send()
     for array in range(3):
         drain(array)
-    store_right.wait()
-    for b in range(nblocks):
-        store_rows(b).wait()
-
-
-def finish(block, acc_hbm, last_hbm, right_hbm, out_hbm, acc, last, right, sems):
-    tile = acc.shape[0] // CHUNKS
-    first_block = jnp.logical_not(lax.axis_index("row") < 2)
-    loads, stores = [], []
-    load_right = pltpu.make_async_copy(right_hbm, right, sems.at[3, 0])
-    load_right.start()
+
+
+def finish(block, acc, last, right, out_hbm, late, sems):
+    stores = []
+    rows = acc.shape[0]
+    early = EARLY * block
+    for i in range(EARLY):
+        part = pl.ds(i * block, block)
+        stores.append(pltpu.make_async_copy(acc.at[part], out_hbm.at[part], sems.at[i]))
+        stores[-1].start()
+    step = (rows - early) // CHUNKS
     for i in range(CHUNKS):
-        part = pl.ds(i * tile, tile)
-        loads.append(
-            (
-                pltpu.make_async_copy(last_hbm.at[:, :, part], last.at[:, :, part], sems.at[0, i]),
-                pltpu.make_async_copy(acc_hbm.at[part], acc.at[part], sems.at[1, i]),
-            )
-        )
-        stores.append(pltpu.make_async_copy(acc.at[part], out_hbm.at[part], sems.at[2, i]))
-        for copy in loads[-1]:
-            copy.start()
-    load_right.wait()
-    for i in range(CHUNKS):
-        part = pl.ds(i * tile, tile)
-        for copy in loads[i]:
-            copy.wait()
-
-        def change():
-            left = jnp.concatenate([last[p, :, part] for p in range(2)], axis=0)
-            acc[part, :] = acc[part, :] - turned_product(left, right[0], right[1])
-
-        if i * tile < block:
-            pl.when(first_block)(change)
-        else:
-            change()
-        stores[i].start()
+        part = pl.ds(early + i * step, step)
+        finish_block(part, False, late, acc, last, right)
+        stores.append(pltpu.make_async_copy(late.at[part], out_hbm.at[part], sems.at[EARLY + i]))
+        stores[-1].start()
     for copy in stores:
         copy.wait()
 
@@ -426,6 +428,7 @@
     hbm = pl.BlockSpec(memory_space=pl.ANY)
     dma = pltpu.SemaphoreType.DMA
     nblocks = rows // block
+    operands = (test_kernel, first_panel.T, second_panel.T, first_inverse, second_inverse)
     acc, last, right = pl.pallas_call(
         kernel,
         out_shape=[
@@ -433,45 +436,42 @@
             jax.ShapeDtypeStruct((2, kc, rows), F32),
             jax.ShapeDtypeStruct((2, 2 * kc, cols), BF16),
         ],
-        in_specs=[hbm, hbm, hbm, vmem, vmem],
-        out_specs=[hbm, hbm, hbm],
+        in_specs=[hbm] * 5,
+        out_specs=[vmem, vmem, vmem],
         scratch_shapes=[
             pltpu.VMEM((2, nz, kc, rows), F32),
             pltpu.VMEM((block, block), F32),
             pltpu.VMEM((block, cols), F32),
             pltpu.VMEM((block, cols), F32),
-            pltpu.VMEM((rows, cols), F32),
+            pltpu.VMEM((block, block), F32),
+            pltpu.VMEM((block, block), F32),
             pltpu.VMEM((block, cols), F32),
             pltpu.VMEM((block, cols), F32),
             pltpu.VMEM((2, block, cols), BF16),
             pltpu.VMEM((2, block, cols), BF16),
             pltpu.VMEM((block, cols), BF16),
             pltpu.VMEM((block, cols), BF16),
-            pltpu.VMEM((2, 2 * kc, cols), BF16),
             dma((2, nz // 2)),
             dma((2, nz // 2, 2 * nblocks)),
             dma((3, 2, 5)),
             dma((3, nz)),
-            dma((4,)),
-            dma((nblocks,)),
+            dma((6,)),
             dma((nblocks,)),
         ],
         compiler_params=pltpu.CompilerParams(
             collective_id=0, has_side_effects=True, vmem_limit_bytes=VMEM_BYTES
         ),
-    )(test_kernel, first_panel.T, second_panel.T, first_inverse, second_inverse)
+    )(*[pltpu.with_memory_space_constraint(v, pltpu.HBM) for v in operands])
     return pl.pallas_call(
         functools.partial(finish, block),
         out_shape=jax.ShapeDtypeStruct((rows, cols), F32),
-        in_specs=[hbm, hbm, hbm],
+        in_specs=[vmem, vmem, vmem],
         out_specs=hbm,
         scratch_shapes=[
             pltpu.VMEM((rows, cols), F32),
-            pltpu.VMEM((2, kc, rows), F32),
-            pltpu.VMEM((2, 2 * kc, cols), BF16),
-            dma((4, CHUNKS)),
+            dma((EARLY + CHUNKS,)),
         ],
-        compiler_params=pltpu.CompilerParams(vmem_limit_bytes=VMEM_BYTES),
+        compiler_params=pltpu.CompilerParams(vmem_limit_bytes=FINISH_BYTES),
     )(acc, last, right)
 
 

time: 96 us -> 92 us (0.958)
  Pallas kernels: 95.7 us -> 91.6 us
    pallas_call x1, Pallas kernels: 4.54 us -> 2.06 us  [per_device(): pl.pallas_call(functools.partial(finish, block), out_shape=jax.ShapeDtype...]
    pallas_call x1, Pallas kernels: 91.2 us -> 89.5 us  [per_device(): pl.pallas_call(kernel, out_shape=[jax.ShapeDtypeStruct((rows, cols), F32)...]
where the time goes in v3:
time: 92 us; the launch traced here: 91.6 us
  Pallas kernels  91.6 us (100%)
    pallas_call x1, Pallas kernels, per_device(): pl.pallas_call(kernel, out_shape=[jax.ShapeDtypeStruct((rows, cols), F32)...  89.5 us
    pallas_call x1, Pallas kernels, per_device(): pl.pallas_call(functools.partial(finish, block), out_shape=jax.ShapeDtype...  2.06 us

profile of v3, /device:TPU:1, one launch (start us, length us, event | category | flops | bytes accessed | tf_op | source)
XLA Modules:
  0.0 91.6 jit_solution(14448625938138061363)
XLA Ops:
  0.0 89.5 %shard_map.55 = (f32[2048,512]{1,0:T(8,128)S(1)}, f32[2,64,2048]{2,1,0:T(8,128)S(1)}, bf16[2,128,512]{2,1,0:T(8,128)(2,1)S(1)}) custom-call(f32[2048,512]{1,0:T(8,128)} %t_hbm.1, f32[64,2048]{1,0:T(8,128)} %bitcast.2, f32[64,2048]{1,0:T(8,128)} %bitcast.3, f32[512,512]{1,0:T(8,128)} %inv1_hbm.1, f32[512,512]{1,0:T(8,128)} %inv2_hbm.1), custom_call_target="tpu_custom_call" | custom-call | tf_op jit(solution)/shard_map/pallas_call | solution.py:432
  89.5 2.1 %shard_map.56 = f32[2048,512]{1,0:T(8,128)} custom-call(f32[2048,512]{1,0:T(8,128)S(1)} %get-tuple-element.8.acc, f32[2,64,2048]{2,1,0:T(8,128)S(1)} %get-tuple-element.9.last, bf16[2,128,512]{2,1,0:T(8,128)(2,1)S(1)} %get-tuple-element.10.right), custom_call_target="tpu_custom_call" | custom-call | tf_op jit(solution)/shard_map/pallas_call | solution.py:465

commit v4 on v3

--- a/solution.py
+++ b/solution.py
@@ -56,7 +56,7 @@
 def kernel(
     t_hbm, p1_hbm, p2_hbm, inv1_hbm, inv2_hbm, acc, last, right,
     pg, pb, t1, t2, inv1, inv2, s1, s2, sh, sl, rh, rl,
-    zs, zr, xs, xr, local, tload,
+    zs, zr, xs, xr, local, tload, ready,
 ):
     nz = pg.shape[1]
     kc = pg.shape[2]
@@ -83,14 +83,16 @@
         return lax.rem(z + (k + nz), nz)
 
     barrier = pltpu.get_barrier_semaphore()
-    neighbours = (
-        (row, origin(1)),
-        (row, origin(-1)),
-        (at(lax.rem(x + 1, NX), y, core), z),
-        (at(lax.rem(x + NX - 1, NX), y, core), z),
-        (at(x, lax.rem(y + 1, NY), core), z),
-        (at(x, lax.rem(y + NY - 1, NY), core), z),
-        (sibling, z),
+
+    def before(k, n):
+        return jnp.where(k == n - 1, 0, k - 1)
+
+    parent = jnp.where(y == 0, at(before(x, NX), y, core), at(x, before(y, NY), core))
+    children = (
+        (jnp.logical_and(y == 0, x <= 1), at(lax.rem(x + 1, NX), y, core)),
+        (source, at(NX - 1, y, core)),
+        (y <= 1, at(x, lax.rem(y + 1, NY), core)),
+        (y == 0, at(x, NY - 1, core)),
     )
 
     def load_rows(b):
@@ -107,9 +109,35 @@
 
     for p in range(2):
         own_panel(p).start()
-    for n in neighbours:
-        pl.semaphore_signal(barrier, inc=1, device_id=n, device_id_type=MESH)
-    pl.semaphore_wait(barrier, len(neighbours))
+    for n in (origin(1), origin(-1)):
+        pl.semaphore_signal(barrier, inc=1, device_id=(row, n), device_id_type=MESH)
+    for sends, target in children:
+        @pl.when(sends)
+        def _():
+            pl.semaphore_signal(barrier, inc=1, device_id=(target, z), device_id_type=MESH)
+
+    @pl.when(core == 0)
+    def _():
+        pl.semaphore_signal(barrier, inc=1, device_id=(sibling, z), device_id_type=MESH)
+
+    pl.semaphore_wait(barrier, 2 + jnp.where(other, 1, 0) + core)
+
+    @pl.when(other)
+    def _():
+        pl.semaphore_signal(ready, inc=1, device_id=(parent, z), device_id_type=MESH)
+
+    @pl.when(core == 1)
+    def _():
+        pl.semaphore_signal(ready, inc=1, device_id=(sibling, z), device_id_type=MESH)
+
+    def wait_receivers():
+        count = 1 - core
+        for sends, _unused in children:
+            count = count + jnp.where(sends, 1, 0)
+
+        @pl.when(count > 0)
+        def _():
+            pl.semaphore_wait(ready, count)
 
     def where(j):
         return j // nblocks, pl.ds((j % nblocks) * block, block)
@@ -172,27 +200,14 @@
         return pltpu.make_async_remote_copy(
             src_ref=src,
             dst_ref=buffers[array].at[piece(array, i)],
-            send_sem=xs.at[array, i % 2, slot],
+            send_sem=xs.at[array, slot],
             recv_sem=xr.at[array, i],
             device_id=(target, z),
             device_id_type=MESH,
         )
 
-    def edges(tree):
-        u, v = x, y
-
-        def to(uu, vv):
-            return at(uu, vv, core)
-
-        return (
-            (jnp.logical_and(v == 0, u <= 1), to(lax.rem(u + 1, NX), v)),
-            (jnp.logical_and(v == 0, u == 0), to(NX - 1, v)),
-            (v <= 1, to(u, lax.rem(v + 1, NX))),
-            (v == 0, to(u, NX - 1)),
-        )
-
     def to_children(array, i, src):
-        for slot, (sends, target) in enumerate(edges(i % 2)):
+        for slot, (sends, target) in enumerate(children):
             @pl.when(sends)
             def _():
                 xcopy(array, i, slot, src, target).start()
@@ -211,23 +226,22 @@
             to_children(array, i, buffers[array].at[piece(array, i)])
 
     def drain(array):
-        pieces = buffers[array].at[pl.ds(0, block // 2)]
-
-        def wait(tree, slot):
+        whole = buffers[array]
+
+        def wait(slot):
             pltpu.make_async_remote_copy(
-                src_ref=pieces, dst_ref=pieces, send_sem=xs.at[array, tree, slot], recv_sem=xr.at[array, 0],
+                src_ref=whole, dst_ref=whole, send_sem=xs.at[array, slot], recv_sem=xr.at[array, 0],
                 device_id=(sibling, z), device_id_type=MESH,
             ).wait_send()
 
         @pl.when(core == min(array, 1))
         def _():
-            for tree in range(2):
-                for slot, (sends, _unused) in enumerate(edges(tree)):
-                    @pl.when(sends)
-                    def _():
-                        wait(tree, slot)
-
-                wait(tree, 4)
+            for slot, (sends, _unused) in enumerate(children):
+                @pl.when(sends)
+                def _():
+                    wait(slot)
+
+            wait(len(children))
 
     def keep_rows(array):
         return pltpu.make_async_copy(t_hbm.at[pl.ds(0, block)], buffers[array], local.at[2])
@@ -261,11 +275,16 @@
             @pl.when(core == array)
             def _():
                 keep_rows(array).start()
+
+        first(0)
+        first(1)
+        wait_receivers()
+        for array in range(2):
+            @pl.when(core == array)
+            def _():
                 for i in range(nz):
                     to_children(array, i, t_hbm.at[pl.ds(i * xp, xp)])
 
-        first(0)
-        first(1)
         start_loads()
         own_panel(0).wait()
         panel_piece(0)
@@ -295,6 +314,7 @@
         for j in range(npieces):
             first(j)
         start_loads()
+        wait_receivers()
         own_panel(0).wait()
         for i in range(nz):
             xforward(0, i)
@@ -316,7 +336,7 @@
 
     @pl.when(source)
     def _():
-        for j in range(1, nblocks):
+        for j in range(1, npieces):
             forward(2, j)
 
         @pl.when(core == 1)
@@ -331,9 +351,8 @@
     @pl.when(other)
     def _():
         for i in range(nz):
+            forward(2, i)
             xforward(2, i)
-            if i >= half:
-                forward(2, i - half)
 
     rh[...], rl[...] = split(t2[...] - turned_product(pb[...], sh[0], sl[0]))
     load_inverse(1).wait()
@@ -352,7 +371,6 @@
     near = (z, origin(-1), origin(1))
     far = (origin(-2), origin(2), origin(-3), origin(3))
     for b in range(nblocks):
-        forward(2, nblocks + b)
         load_rows(b).wait()
         update(b, near)
 
@@ -453,10 +471,11 @@
             pltpu.VMEM((block, cols), BF16),
             dma((2, nz // 2)),
             dma((2, nz // 2, 2 * nblocks)),
-            dma((3, 2, 5)),
+            dma((3, 5)),
             dma((3, nz)),
             dma((6,)),
             dma((nblocks,)),
+            pltpu.SemaphoreType.REGULAR,
         ],
         compiler_params=pltpu.CompilerParams(
             collective_id=0, has_side_effects=True, vmem_limit_bytes=VMEM_BYTES

time: 92 us -> 89.4 us (0.972)
  Pallas kernels: 91.6 us -> 89.3 us
    pallas_call x1, Pallas kernels: 89.5 us -> 87.2 us  [per_device(): pl.pallas_call(kernel, out_shape=[jax.ShapeDtypeStruct((rows, cols), F32)...]
where the time goes in v4:
time: 89.4 us; the launch traced here: 89.3 us
  Pallas kernels  89.3 us (100%)
    pallas_call x1, Pallas kernels, per_device(): pl.pallas_call(kernel, out_shape=[jax.ShapeDtypeStruct((rows, cols), F32)...  87.2 us
    pallas_call x1, Pallas kernels, per_device(): pl.pallas_call(functools.partial(finish, block), out_shape=jax.ShapeDtype...  2.06 us

profile of v4, /device:TPU:1, one launch (start us, length us, event | category | flops | bytes accessed | tf_op | source)
XLA Modules:
  0.0 89.3 jit_solution(3183416568478860588)
XLA Ops:
  0.0 87.2 %shard_map.55 = (f32[2048,512]{1,0:T(8,128)S(1)}, f32[2,64,2048]{2,1,0:T(8,128)S(1)}, bf16[2,128,512]{2,1,0:T(8,128)(2,1)S(1)}) custom-call(f32[2048,512]{1,0:T(8,128)} %t_hbm.1, f32[64,2048]{1,0:T(8,128)} %bitcast.2, f32[64,2048]{1,0:T(8,128)} %bitcast.3, f32[512,512]{1,0:T(8,128)} %inv1_hbm.1, f32[512,512]{1,0:T(8,128)} %inv2_hbm.1), custom_call_target="tpu_custom_call" | custom-call | tf_op jit(solution)/shard_map/pallas_call | solution.py:450
  87.2 2.1 %shard_map.56 = f32[2048,512]{1,0:T(8,128)} custom-call(f32[2048,512]{1,0:T(8,128)S(1)} %get-tuple-element.8.acc, f32[2,64,2048]{2,1,0:T(8,128)S(1)} %get-tuple-element.9.last, bf16[2,128,512]{2,1,0:T(8,128)(2,1)S(1)} %get-tuple-element.10.right), custom_call_target="tpu_custom_call" | custom-call | tf_op jit(solution)/shard_map/pallas_call | solution.py:484

commit v5 on v4

--- a/solution.py
+++ b/solution.py
@@ -56,7 +56,7 @@
 def kernel(
     t_hbm, p1_hbm, p2_hbm, inv1_hbm, inv2_hbm, acc, last, right,
     pg, pb, t1, t2, inv1, inv2, s1, s2, sh, sl, rh, rl,
-    zs, zr, xs, xr, local, tload, ready,
+    zs, zr, xs, xr, local, tload, ready, below,
 ):
     nz = pg.shape[1]
     kc = pg.shape[2]
@@ -109,8 +109,7 @@
 
     for p in range(2):
         own_panel(p).start()
-    for n in (origin(1), origin(-1)):
-        pl.semaphore_signal(barrier, inc=1, device_id=(row, n), device_id_type=MESH)
+    pl.semaphore_signal(barrier, inc=1, device_id=(row, origin(-1)), device_id_type=MESH)
     for sends, target in children:
         @pl.when(sends)
         def _():
@@ -120,7 +119,8 @@
     def _():
         pl.semaphore_signal(barrier, inc=1, device_id=(sibling, z), device_id_type=MESH)
 
-    pl.semaphore_wait(barrier, 2 + jnp.where(other, 1, 0) + core)
+    pl.semaphore_wait(barrier, 1 + jnp.where(other, 1, 0) + core)
+    pl.semaphore_signal(below, inc=1, device_id=(row, origin(1)), device_id_type=MESH)
 
     @pl.when(other)
     def _():
@@ -181,6 +181,13 @@
         for side in SIDES:
             zsend(side, 1, j)
 
+    def start(count):
+        for j in range(count):
+            zsend(0, 1, j)
+        pl.semaphore_wait(below, 1)
+        for j in range(count):
+            zsend(1, 1, j)
+
     def forward(h, j):
         for side in SIDES:
             zwait(side, h, j)
@@ -276,8 +283,7 @@
             def _():
                 keep_rows(array).start()
 
-        first(0)
-        first(1)
+        start(2)
         wait_receivers()
         for array in range(2):
             @pl.when(core == array)
@@ -311,8 +317,7 @@
 
     @pl.when(other)
     def _():
-        for j in range(npieces):
-            first(j)
+        start(npieces)
         start_loads()
         wait_receivers()
         own_panel(0).wait()
@@ -476,6 +481,7 @@
             dma((6,)),
             dma((nblocks,)),
             pltpu.SemaphoreType.REGULAR,
+            pltpu.SemaphoreType.REGULAR,
         ],
         compiler_params=pltpu.CompilerParams(
             collective_id=0, has_side_effects=True, vmem_limit_bytes=VMEM_BYTES

time: 89.4 us -> 89.4 us (level)
  no operation moved by 1% of the time
where the time goes in v5:
time: 89.4 us
  Pallas kernels  89.4 us (100%)
    pallas_call x1, Pallas kernels, per_device(): pl.pallas_call(kernel, out_shape=[jax.ShapeDtypeStruct((rows, cols), F32)...  87.3 us
    pallas_call x1, Pallas kernels, per_device(): pl.pallas_call(functools.partial(finish, block), out_shape=jax.ShapeDtype...  2.06 us

profile of v5, /device:TPU:1, one launch (start us, length us, event | category | flops | bytes accessed | tf_op | source)
XLA Modules:
  0.0 89.4 jit_solution(5437350261601583570)
XLA Ops:
  0.0 87.3 %shard_map.55 = (f32[2048,512]{1,0:T(8,128)S(1)}, f32[2,64,2048]{2,1,0:T(8,128)S(1)}, bf16[2,128,512]{2,1,0:T(8,128)(2,1)S(1)}) custom-call(f32[2048,512]{1,0:T(8,128)} %t_hbm.1, f32[64,2048]{1,0:T(8,128)} %bitcast.2, f32[64,2048]{1,0:T(8,128)} %bitcast.3, f32[512,512]{1,0:T(8,128)} %inv1_hbm.1, f32[512,512]{1,0:T(8,128)} %inv2_hbm.1), custom_call_target="tpu_custom_call" | custom-call | tf_op jit(solution)/shard_map/pallas_call | solution.py:455
  87.3 2.1 %shard_map.56 = f32[2048,512]{1,0:T(8,128)} custom-call(f32[2048,512]{1,0:T(8,128)S(1)} %get-tuple-element.8.acc, f32[2,64,2048]{2,1,0:T(8,128)S(1)} %get-tuple-element.9.last, bf16[2,128,512]{2,1,0:T(8,128)(2,1)S(1)} %get-tuple-element.10.right), custom_call_target="tpu_custom_call" | custom-call | tf_op jit(solution)/shard_map/pallas_call | solution.py:490

commit v6 on v5

--- a/solution.py
+++ b/solution.py
@@ -63,7 +63,7 @@
     half = nz // 2
     block = t1.shape[0]
     nblocks = acc.shape[0] // block
-    npieces = 2 * nblocks
+    npieces = nblocks + nblocks // 2
     xp = block // nz
     row = lax.axis_index("row")
     z = lax.axis_index("col")
@@ -107,8 +107,6 @@
     def load_inverse(p):
         return pltpu.make_async_copy(*inverses[p], local.at[4 + p])
 
-    for p in range(2):
-        own_panel(p).start()
     pl.semaphore_signal(barrier, inc=1, device_id=(row, origin(-1)), device_id_type=MESH)
     for sends, target in children:
         @pl.when(sends)
@@ -122,13 +120,14 @@
     pl.semaphore_wait(barrier, 1 + jnp.where(other, 1, 0) + core)
     pl.semaphore_signal(below, inc=1, device_id=(row, origin(1)), device_id_type=MESH)
 
-    @pl.when(other)
-    def _():
-        pl.semaphore_signal(ready, inc=1, device_id=(parent, z), device_id_type=MESH)
-
-    @pl.when(core == 1)
-    def _():
-        pl.semaphore_signal(ready, inc=1, device_id=(sibling, z), device_id_type=MESH)
+    def answer():
+        @pl.when(other)
+        def _():
+            pl.semaphore_signal(ready, inc=1, device_id=(parent, z), device_id_type=MESH)
+
+        @pl.when(core == 1)
+        def _():
+            pl.semaphore_signal(ready, inc=1, device_id=(sibling, z), device_id_type=MESH)
 
     def wait_receivers():
         count = 1 - core
@@ -140,7 +139,12 @@
             pl.semaphore_wait(ready, count)
 
     def where(j):
-        return j // nblocks, pl.ds((j % nblocks) * block, block)
+        if j < nblocks:
+            return 0, pl.ds(j * block, block)
+        return 1, pl.ds((j - nblocks) * 2 * block, 2 * block)
+
+    def second(b):
+        return nblocks + b // 2
 
     def hops(side, j):
         return half if (j % 2 == side) else half - 1
@@ -184,6 +188,9 @@
     def start(count):
         for j in range(count):
             zsend(0, 1, j)
+        answer()
+        for p in range(2):
+            own_panel(p).start()
         pl.semaphore_wait(below, 1)
         for j in range(count):
             zsend(1, 1, j)
@@ -356,7 +363,8 @@
     @pl.when(other)
     def _():
         for i in range(nz):
-            forward(2, i)
+            if i < npieces:
+                forward(2, i)
             xforward(2, i)
 
     rh[...], rl[...] = split(t2[...] - turned_product(pb[...], sh[0], sl[0]))
@@ -379,15 +387,16 @@
         load_rows(b).wait()
         update(b, near)
 
-    for j in range(npieces):
-        if j == 0:
-            @pl.when(other)
-            def _():
-                forward(half - 1, 0)
-        else:
-            forward(half - 1, j)
-        if j >= nblocks:
-            b = j - nblocks
+    for pair in range(nblocks // 2):
+        b = 2 * pair
+        for k in (b, b + 1, second(b)) if b < EARLY else (b + 1, b, second(b)):
+            if k == 0:
+                @pl.when(other)
+                def _():
+                    forward(half - 1, 0)
+            else:
+                forward(half - 1, k)
+        for b in (2 * pair, 2 * pair + 1):
             update(b, far)
             if b == 0:
                 @pl.when(row == 0)
@@ -403,7 +412,7 @@
         right[0, pl.ds(p * kc, kc), :] = sh[p, final, :]
         right[1, pl.ds(p * kc, kc), :] = sl[p, final, :]
     for b in range(nblocks):
-        for j in (b, b + nblocks):
+        for j in (b, second(b)) if b % 2 == 0 else (b,):
             for side in SIDES:
                 if j == 0:
                     @pl.when(other)

time: 89.4 us -> 89.6 us (level)
  no operation moved by 1% of the time
where the time goes in v6:
time: 89.6 us; the launch traced here: 89.4 us
  Pallas kernels  89.4 us (100%)
    pallas_call x1, Pallas kernels, per_device(): pl.pallas_call(kernel, out_shape=[jax.ShapeDtypeStruct((rows, cols), F32)...  87.3 us
    pallas_call x1, Pallas kernels, per_device(): pl.pallas_call(functools.partial(finish, block), out_shape=jax.ShapeDtype...  2.06 us

profile of v6, /device:TPU:1, one launch (start us, length us, event | category | flops | bytes accessed | tf_op | source)
XLA Modules:
  0.0 89.4 jit_solution(16792999481389223114)
XLA Ops:
  0.0 87.3 %shard_map.55 = (f32[2048,512]{1,0:T(8,128)S(1)}, f32[2,64,2048]{2,1,0:T(8,128)S(1)}, bf16[2,128,512]{2,1,0:T(8,128)(2,1)S(1)}) custom-call(f32[2048,512]{1,0:T(8,128)} %t_hbm.1, f32[64,2048]{1,0:T(8,128)} %bitcast.2, f32[64,2048]{1,0:T(8,128)} %bitcast.3, f32[512,512]{1,0:T(8,128)} %inv1_hbm.1, f32[512,512]{1,0:T(8,128)} %inv2_hbm.1), custom_call_target="tpu_custom_call" | custom-call | tf_op jit(solution)/shard_map/pallas_call | solution.py:464
  87.3 2.1 %shard_map.56 = f32[2048,512]{1,0:T(8,128)} custom-call(f32[2048,512]{1,0:T(8,128)S(1)} %get-tuple-element.8.acc, f32[2,64,2048]{2,1,0:T(8,128)S(1)} %get-tuple-element.9.last, bf16[2,128,512]{2,1,0:T(8,128)(2,1)S(1)} %get-tuple-element.10.right), custom_call_target="tpu_custom_call" | custom-call | tf_op jit(solution)/shard_map/pallas_call | solution.py:499

commit v7 on v6

--- a/solution.py
+++ b/solution.py
@@ -15,7 +15,7 @@
 VMEM_BYTES = 36 * 1024 * 1024
 FINISH_BYTES = 12 * 1024 * 1024
 EARLY = 2
-CHUNKS = 4
+CHUNKS = 2
 
 
 def split(value):

time: 89.6 us -> 89.6 us (level)
  no operation moved by 1% of the time
where the time goes in v7:
time: 89.6 us; the launch traced here: 89.4 us
  Pallas kernels  89.4 us (100%)
    pallas_call x1, Pallas kernels, per_device(): pl.pallas_call(kernel, out_shape=[jax.ShapeDtypeStruct((rows, cols), F32)...  87.3 us
    pallas_call x1, Pallas kernels, per_device(): pl.pallas_call(functools.partial(finish, block), out_shape=jax.ShapeDtype...  2.04 us

profile of v7, /device:TPU:1, one launch (start us, length us, event | category | flops | bytes accessed | tf_op | source)
XLA Modules:
  0.0 89.4 jit_solution(16826596912895096528)
XLA Ops:
  0.0 87.3 %shard_map.55 = (f32[2048,512]{1,0:T(8,128)S(1)}, f32[2,64,2048]{2,1,0:T(8,128)S(1)}, bf16[2,128,512]{2,1,0:T(8,128)(2,1)S(1)}) custom-call(f32[2048,512]{1,0:T(8,128)} %t_hbm.1, f32[64,2048]{1,0:T(8,128)} %bitcast.2, f32[64,2048]{1,0:T(8,128)} %bitcast.3, f32[512,512]{1,0:T(8,128)} %inv1_hbm.1, f32[512,512]{1,0:T(8,128)} %inv2_hbm.1), custom_call_target="tpu_custom_call" | custom-call | tf_op jit(solution)/shard_map/pallas_call | solution.py:464
  87.3 2.0 %shard_map.56 = f32[2048,512]{1,0:T(8,128)} custom-call(f32[2048,512]{1,0:T(8,128)S(1)} %get-tuple-element.8.acc, f32[2,64,2048]{2,1,0:T(8,128)S(1)} %get-tuple-element.9.last, bf16[2,128,512]{2,1,0:T(8,128)(2,1)S(1)} %get-tuple-element.10.right), custom_call_target="tpu_custom_call" | custom-call | tf_op jit(solution)/shard_map/pallas_call | solution.py:499
